TPU v7x, 32 devices: a whole 2x2x4 slice. The times are simulated.
32 devices in a mesh: lat: 4 (over x, core), lon: 8 (over z, y).
Axes of the slice: x: 2, y: 2, z: 4, core: 2. Of those that a mesh axis runs over, the one named last changes fastest.
Arguments:
- ensemble: bfloat16 [1920, 32, 1024], P(('lat', 'lon')), may hold values from -48 to 48
- obs_interp: bfloat16 [4, 8, 64, 4, 128], P('lat', 'lon'), may hold values from 0.049804688 to 1
- obs_start: int32 [4, 8, 64, 128], P('lat', 'lon'), may hold values from 0 to 124
- obs_levels: bfloat16 [4, 8, 64, 24, 128], P('lat', 'lon'), may hold values from -1.25 to 1.25
- obs_values: float32 [4, 8, 64, 128], P('lat', 'lon'), may hold values from -40 to 40
- obs_weight: float32 [4, 8, 64, 128], P('lat', 'lon'), may hold values from 0.001953125 to 0.00390625
- obs_rows: int32 [4, 8, 64], P('lat', 'lon'), may hold values from 0 to 7
- obs_count: int32 [4, 8], P('lat', 'lon'), may hold values from 8 to 64, as said below
- local_mask: int32 [4, 8, 8, 9], P('lat', 'lon'), may hold values 0 or 1
Outputs:
- analysis: bfloat16 [80, 24, 32, 1024], P(None, None, 'lat', 'lon')
Inputs may be any that keep to these rules, and one draw needn't show every extreme that they name: `obs_count`: blocks from this slot on are ignored; some tile has 64 live blocks.
All inputs are finite; a program needn't handle non-finite values. No bound on the sum of `local_mask` on one device may be relied on, other than what follows from the above.
Results may differ from a plain program's by a relative error of at most 0.005.
Values may be sent and summed in bfloat16 or wider, within the bound.
A program may use at most 64 MiB of HBM per device.

v0:
```python
import jax
import jax.numpy as jnp
from jax import lax
from jax.sharding import PartitionSpec as P

NS_ITERS = 6


HIGHEST_PRECISION = lax.Precision.HIGHEST


def padded(shard, sides, width, wrap):
    for axis, dim in sides:
        devices, length = (lax.axis_size(axis), shard.shape[dim])
        up = [(i, (i + 1) % devices) for i in range(devices if wrap else devices - 1)]
        down = [(j, i) for i, j in up]
        last = lax.slice_in_dim(shard, length - width, length, axis=dim)
        leading = lax.slice_in_dim(shard, 0, width, axis=dim)
        before = lax.ppermute(last, axis, up)
        after = lax.ppermute(leading, axis, down)
        shard = jnp.concatenate([before, shard, after], axis=dim)
    return shard


def passed_along(block, axis, distance):
    devices = range(lax.axis_size(axis))
    route = [((i - distance) % len(devices), i) for i in devices]
    return lax.ppermute(block, axis, route)


def ensemble_transform(summed, members):
    identity = jnp.eye(members, dtype=jnp.float32)
    system = (members - 1) * identity + summed[:, :, :members]
    target = summed[:, :, members]
    scale = jnp.sqrt(jnp.sum(system * system, axis=(1, 2)))
    root_term = system / scale[:, None, None]
    inverse = jnp.broadcast_to(identity, system.shape)
    for repeat in range(NS_ITERS):
        middle = 1.5 * identity - 0.5 * jnp.einsum(
            "bij,bjk->bik", inverse, root_term, precision=HIGHEST_PRECISION
        )
        root_term = jnp.einsum("bij,bjk->bik", root_term, middle, precision=HIGHEST_PRECISION)
        inverse = jnp.einsum("bij,bjk->bik", middle, inverse, precision=HIGHEST_PRECISION)
    half_step = jnp.einsum("bij,bj->bi", inverse, target, precision=HIGHEST_PRECISION)
    shift_mean = (
        jnp.einsum("bij,bj->bi", inverse, half_step, precision=HIGHEST_PRECISION) / scale[:, None]
    )
    spread = jnp.sqrt(jnp.float32(members - 1)) * inverse / jnp.sqrt(scale)[:, None, None]
    return (spread + shift_mean[:, :, None]).astype(jnp.bfloat16)


def stencil_matrix(weights, starts, width):
    columns = jnp.arange(width, dtype=jnp.int32)
    dense = jnp.zeros(starts.shape + (width,), jnp.bfloat16)
    for offset in range(weights.shape[1]):
        hit = starts[:, :, None] + offset == columns[None, None, :]
        dense = dense + jnp.where(hit, weights[:, offset, :, None], jnp.zeros((), jnp.bfloat16))
    return dense


def per_device(
    ensemble,
    obs_interp,
    obs_start,
    obs_levels,
    obs_values,
    obs_weight,
    obs_rows,
    obs_count,
    local_mask,
):
    lat_tiles = lax.axis_size("lat")
    lon_tiles = lax.axis_size("lon")
    lat_here = lax.axis_index("lat")
    field_share, grid_rows, grid_cols = ensemble.shape
    tile_rows = grid_rows // lat_tiles
    tile_cols = grid_cols // lon_tiles
    block_slots, level_count, obs_slots = obs_levels.shape[2:]
    members = field_share * lat_tiles * lon_tiles // level_count
    layered = ensemble.reshape(field_share, lat_tiles, tile_rows, lon_tiles, tile_cols)
    ordered = jnp.transpose(layered, (0, 1, 3, 2, 4)).reshape(
        field_share, lat_tiles * lon_tiles, tile_rows, tile_cols
    )
    arrived = lax.all_to_all(ordered, ("lat", "lon"), split_axis=1, concat_axis=0, tiled=True)
    tile_state = arrived.reshape(members, level_count, tile_rows, tile_cols)
    ens_mean = jnp.sum(tile_state, axis=0, dtype=jnp.float32) / members
    deviation = (tile_state - ens_mean).astype(jnp.bfloat16)
    interp = obs_interp[0, 0]
    starts = obs_start[0, 0]
    levels = obs_levels[0, 0]
    values = obs_values[0, 0]
    weights = obs_weight[0, 0]
    block_rows = obs_rows[0, 0]
    live_count = obs_count[0, 0]
    group_total = block_slots // 8

    def project_group(group_index):
        first_slot = group_index * 8
        group_rows = lax.dynamic_slice_in_dim(block_rows, first_slot, 8)
        picked = jnp.take(tile_state, group_rows, axis=2)
        group_interp = lax.dynamic_slice_in_dim(interp, first_slot, 8, 0)
        group_starts = lax.dynamic_slice_in_dim(starts, first_slot, 8, 0)
        dense = stencil_matrix(group_interp, group_starts, tile_cols)
        group_levels = lax.dynamic_slice_in_dim(levels, first_slot, 8, 0).astype(jnp.float32)
        projected = jnp.einsum("kfjc,joc->kfjo", picked, dense, preferred_element_type=jnp.float32)
        return jnp.sum(projected * jnp.transpose(group_levels, (1, 0, 2))[None], axis=1)

    def add_group(group_index, obs_total):
        return lax.dynamic_update_slice_in_dim(
            obs_total, project_group(group_index), group_index * 8, 1
        )

    empty_obs = jnp.zeros((members, block_slots, obs_slots), jnp.float32)
    obs_ens = lax.fori_loop(0, group_total, add_group, empty_obs)
    obs_mean = jnp.mean(obs_ens, axis=0)
    obs_dev = obs_ens - obs_mean
    innov = values - obs_mean
    is_live = jnp.arange(block_slots, dtype=jnp.int32)[:, None] < live_count
    live = jnp.where(is_live, weights, jnp.zeros_like(weights))
    flat_dev = obs_dev.reshape(members, -1)
    paired = jnp.concatenate([flat_dev.T, innov.reshape(-1, 1)], axis=1)
    partial_value = jnp.dot(flat_dev * live.reshape(1, -1), paired, precision=HIGHEST_PRECISION)
    lon_stack = padded(partial_value[None], (("lon", 0),), 1, True)
    lat_stack = padded(lon_stack[None], (("lat", 0),), 1, False)
    across = passed_along(lon_stack, "lon", lon_tiles // 2)
    mirrored = across[::-1]
    north_rows = jnp.where(lat_here == 0, mirrored, lat_stack[0])
    slot_sums = jnp.stack([north_rows, lat_stack[1], lat_stack[2]]).reshape(
        9, members * (members + 1)
    )
    slot_mask = local_mask[0, 0].astype(jnp.float32)
    summed = jnp.dot(slot_mask, slot_sums, precision=HIGHEST_PRECISION).reshape(
        tile_rows, members, members + 1
    )
    transform = ensemble_transform(summed, members)
    update = jnp.einsum("kfbc,bkl->lfbc", deviation, transform, preferred_element_type=jnp.float32)
    return (ens_mean[None] + update).astype(jnp.bfloat16)


def solution(mesh):
    placed = (
        P(("lat", "lon"), None, None),
        P("lat", "lon", None, None, None),
        P("lat", "lon", None, None),
        P("lat", "lon", None, None, None),
        P("lat", "lon", None, None),
        P("lat", "lon", None, None),
        P("lat", "lon", None),
        P("lat", "lon"),
        P("lat", "lon", None, None),
    )
    return jax.shard_map(
        per_device,
        mesh=mesh,
        in_specs=placed,
        out_specs=P(None, None, "lat", "lon"),
        check_vma=False,
    )
```

profile of v0, /device:TPU:0, one launch (start us, length us, event | category | flops | bytes accessed | tf_op | source)
XLA Modules:
  0.0 274.0 jit_solution(8996412760952379175)
XLA Ops:
  0.0 4.7 %copy.32 = bf16[60,4,8,8,128]{4,2,0,3,1:T(8,128)(2,1)} copy(bf16[60,4,8,8,128]{4,2,3,1,0:T(8,128)(2,1)} %bitcast.138) | data formatting | bytes 7864320 | tf_op jit(solution)/shard_map/reshape | solution.py:80
  4.7 7.4 %all-to-all-start = ((bf16[60,32,8,128]{3,2,0,1:T(8,128)(2,1)}), bf16[60,32,8,128]{3,2,0,1:T(8,128)(2,1)}, u32[]{:S(2)}, u32[]{:S(2)}) async-start(bf16[60,32,8,128]{3,2,0,1:T(8,128)(2,1)} %bitcast.137), calls=%async_computation | async-start | bytes 7864320 | tf_op jit(solution)/shard_map/all_to_all | solution.py:84
  13.0 89.2 %all-to-all-done = bf16[60,32,8,128]{3,2,0,1:T(8,128)(2,1)} async-done(((bf16[60,32,8,128]{3,2,0,1:T(8,128)(2,1)}), bf16[60,32,8,128]{3,2,0,1:T(8,128)(2,1)}, u32[]{:S(2)}, u32[]{:S(2)}) %all-to-all-start) | async-done | bytes 3932192 | tf_op jit(solution)/shard_map/all_to_all | solution.py:84
  102.2 5.2 %copy.35 = bf16[80,24,8,128]{3,1,2,0:T(8,128)(2,1)} copy(bf16[80,24,8,128]{3,2,1,0:T(8,128)(2,1)} %bitcast.14) | data formatting | bytes 7864320 | tf_op jit(solution)/shard_map/while | solution.py:114
  107.6 122.9 %while.13 = (s32[]{:T(128)}, f32[80,64,128]{2,0,1:T(8,128)S(1)}, s32[64,128]{1,0:T(8,128)}, bf16[64,4,128]{2,0,1:T(8,128)(2,1)S(1)}, s32[64]{0:T(128)S(1)}, /*in...) while((s32[]{:T(128)}, f32[80,64,128]{2,0,1:T(8,128)S(1)}, ...), condition=%wide.region_3.4_spmd, body=%wide.region_1.3_spmd.sunk | while | flops 511258688 | bytes 20959624 | solution.py:114
  107.7 5.1 %gather_fusion = bf16[8,80,24,128]{3,2,1,0:T(8,128)(2,1)} fusion(bf16[80,24,8,128]{3,1,2,0:T(8,128)(2,1)} %get-tuple-element.284, s32[1024]{0:T(1024)S(1)} %pad_clamp_fusion.2), kind=kCustom, calls=%fused_computation.clone.1 | custom fusion | bytes 7864352 | tf_op jit(solution)/shard_map/while/body/eval_jaxpr/jit(_take)/gather | solution.py:100
  112.8 4.4 %select_bitcast_fusion.2 = bf16[80,24,8,128]{3,1,0,2:T(8,128)(2,1)} fusion(bf16[8,80,24,128]{3,2,1,0:T(8,128)(2,1)} %gather_fusion, pred[8]{0:T(512)(128)(4,1)S(1)} %get-tuple-element.242), kind=kLoop, calls=%fused_computation.5.clone.1 | loop fusion | flops 1966080 | bytes 7864328 | tf_op jit(solution)/shard_map/while/body/eval_jaxpr/jit(_take)/select_n | solution.py:100
  118.8 4.1 %fusion.119 = f32[80,8,128]{2,0,1:T(8,128)S(1)} fusion(f32[24,8,128]{2,0,1:T(8,128)S(1)} %convert_bitcast_fusion.2, bf16[80,24,8,128]{3,1,0,2:T(8,128)(2,1)} %select_bitcast_fusion.2, s32[8,128]{1,0:T(8,128)S(1)} %get-tuple-element.244, s32[8,128]{1,0:T(8,128)S(1)} %get-tuple-element.245, s32[8,128]{1,0:T(8,128)S(1)} %get-tuple-element.246, ...), kind=kOutput, calls=%fused_computation.2.clone.1 | convolution fusion | flops 509263872 | bytes 4382720 | tf_op jit(solution)/shard_map/while/body/eval_jaxpr/kfjc,joc->kfjo/dot_general | solution.py:105
  123.1 5.1 %gather_fusion = bf16[8,80,24,128]{3,2,1,0:T(8,128)(2,1)} fusion(bf16[80,24,8,128]{3,1,2,0:T(8,128)(2,1)} %get-tuple-element.284, s32[1024]{0:T(1024)S(1)} %pad_clamp_fusion.2), kind=kCustom, calls=%fused_computation.clone.1 | custom fusion | bytes 7864352 | tf_op jit(solution)/shard_map/while/body/eval_jaxpr/jit(_take)/gather | solution.py:100
  128.2 4.4 %select_bitcast_fusion.2 = bf16[80,24,8,128]{3,1,0,2:T(8,128)(2,1)} fusion(bf16[8,80,24,128]{3,2,1,0:T(8,128)(2,1)} %gather_fusion, pred[8]{0:T(512)(128)(4,1)S(1)} %get-tuple-element.242), kind=kLoop, calls=%fused_computation.5.clone.1 | loop fusion | flops 1966080 | bytes 7864328 | tf_op jit(solution)/shard_map/while/body/eval_jaxpr/jit(_take)/select_n | solution.py:100
  134.1 4.1 %fusion.119 = f32[80,8,128]{2,0,1:T(8,128)S(1)} fusion(f32[24,8,128]{2,0,1:T(8,128)S(1)} %convert_bitcast_fusion.2, bf16[80,24,8,128]{3,1,0,2:T(8,128)(2,1)} %select_bitcast_fusion.2, s32[8,128]{1,0:T(8,128)S(1)} %get-tuple-element.244, s32[8,128]{1,0:T(8,128)S(1)} %get-tuple-element.245, s32[8,128]{1,0:T(8,128)S(1)} %get-tuple-element.246, ...), kind=kOutput, calls=%fused_computation.2.clone.1 | convolution fusion | flops 509263872 | bytes 4382720 | tf_op jit(solution)/shard_map/while/body/eval_jaxpr/kfjc,joc->kfjo/dot_general | solution.py:105
  138.4 5.1 %gather_fusion = bf16[8,80,24,128]{3,2,1,0:T(8,128)(2,1)} fusion(bf16[80,24,8,128]{3,1,2,0:T(8,128)(2,1)} %get-tuple-element.284, s32[1024]{0:T(1024)S(1)} %pad_clamp_fusion.2), kind=kCustom, calls=%fused_computation.clone.1 | custom fusion | bytes 7864352 | tf_op jit(solution)/shard_map/while/body/eval_jaxpr/jit(_take)/gather | solution.py:100
  143.5 4.4 %select_bitcast_fusion.2 = bf16[80,24,8,128]{3,1,0,2:T(8,128)(2,1)} fusion(bf16[8,80,24,128]{3,2,1,0:T(8,128)(2,1)} %gather_fusion, pred[8]{0:T(512)(128)(4,1)S(1)} %get-tuple-element.242), kind=kLoop, calls=%fused_computation.5.clone.1 | loop fusion | flops 1966080 | bytes 7864328 | tf_op jit(solution)/shard_map/while/body/eval_jaxpr/jit(_take)/select_n | solution.py:100
  149.5 4.1 %fusion.119 = f32[80,8,128]{2,0,1:T(8,128)S(1)} fusion(f32[24,8,128]{2,0,1:T(8,128)S(1)} %convert_bitcast_fusion.2, bf16[80,24,8,128]{3,1,0,2:T(8,128)(2,1)} %select_bitcast_fusion.2, s32[8,128]{1,0:T(8,128)S(1)} %get-tuple-element.244, s32[8,128]{1,0:T(8,128)S(1)} %get-tuple-element.245, s32[8,128]{1,0:T(8,128)S(1)} %get-tuple-element.246, ...), kind=kOutput, calls=%fused_computation.2.clone.1 | convolution fusion | flops 509263872 | bytes 4382720 | tf_op jit(solution)/shard_map/while/body/eval_jaxpr/kfjc,joc->kfjo/dot_general | solution.py:105
  153.8 5.1 %gather_fusion = bf16[8,80,24,128]{3,2,1,0:T(8,128)(2,1)} fusion(bf16[80,24,8,128]{3,1,2,0:T(8,128)(2,1)} %get-tuple-element.284, s32[1024]{0:T(1024)S(1)} %pad_clamp_fusion.2), kind=kCustom, calls=%fused_computation.clone.1 | custom fusion | bytes 7864352 | tf_op jit(solution)/shard_map/while/body/eval_jaxpr/jit(_take)/gather | solution.py:100
  158.9 4.4 %select_bitcast_fusion.2 = bf16[80,24,8,128]{3,1,0,2:T(8,128)(2,1)} fusion(bf16[8,80,24,128]{3,2,1,0:T(8,128)(2,1)} %gather_fusion, pred[8]{0:T(512)(128)(4,1)S(1)} %get-tuple-element.242), kind=kLoop, calls=%fused_computation.5.clone.1 | loop fusion | flops 1966080 | bytes 7864328 | tf_op jit(solution)/shard_map/while/body/eval_jaxpr/jit(_take)/select_n | solution.py:100
  164.8 4.1 %fusion.119 = f32[80,8,128]{2,0,1:T(8,128)S(1)} fusion(f32[24,8,128]{2,0,1:T(8,128)S(1)} %convert_bitcast_fusion.2, bf16[80,24,8,128]{3,1,0,2:T(8,128)(2,1)} %select_bitcast_fusion.2, s32[8,128]{1,0:T(8,128)S(1)} %get-tuple-element.244, s32[8,128]{1,0:T(8,128)S(1)} %get-tuple-element.245, s32[8,128]{1,0:T(8,128)S(1)} %get-tuple-element.246, ...), kind=kOutput, calls=%fused_computation.2.clone.1 | convolution fusion | flops 509263872 | bytes 4382720 | tf_op jit(solution)/shard_map/while/body/eval_jaxpr/kfjc,joc->kfjo/dot_general | solution.py:105
  169.1 5.1 %gather_fusion = bf16[8,80,24,128]{3,2,1,0:T(8,128)(2,1)} fusion(bf16[80,24,8,128]{3,1,2,0:T(8,128)(2,1)} %get-tuple-element.284, s32[1024]{0:T(1024)S(1)} %pad_clamp_fusion.2), kind=kCustom, calls=%fused_computation.clone.1 | custom fusion | bytes 7864352 | tf_op jit(solution)/shard_map/while/body/eval_jaxpr/jit(_take)/gather | solution.py:100
  174.3 4.4 %select_bitcast_fusion.2 = bf16[80,24,8,128]{3,1,0,2:T(8,128)(2,1)} fusion(bf16[8,80,24,128]{3,2,1,0:T(8,128)(2,1)} %gather_fusion, pred[8]{0:T(512)(128)(4,1)S(1)} %get-tuple-element.242), kind=kLoop, calls=%fused_computation.5.clone.1 | loop fusion | flops 1966080 | bytes 7864328 | tf_op jit(solution)/shard_map/while/body/eval_jaxpr/jit(_take)/select_n | solution.py:100
  180.2 4.1 %fusion.119 = f32[80,8,128]{2,0,1:T(8,128)S(1)} fusion(f32[24,8,128]{2,0,1:T(8,128)S(1)} %convert_bitcast_fusion.2, bf16[80,24,8,128]{3,1,0,2:T(8,128)(2,1)} %select_bitcast_fusion.2, s32[8,128]{1,0:T(8,128)S(1)} %get-tuple-element.244, s32[8,128]{1,0:T(8,128)S(1)} %get-tuple-element.245, s32[8,128]{1,0:T(8,128)S(1)} %get-tuple-element.246, ...), kind=kOutput, calls=%fused_computation.2.clone.1 | convolution fusion | flops 509263872 | bytes 4382720 | tf_op jit(solution)/shard_map/while/body/eval_jaxpr/kfjc,joc->kfjo/dot_general | solution.py:105
  184.5 5.1 %gather_fusion = bf16[8,80,24,128]{3,2,1,0:T(8,128)(2,1)} fusion(bf16[80,24,8,128]{3,1,2,0:T(8,128)(2,1)} %get-tuple-element.284, s32[1024]{0:T(1024)S(1)} %pad_clamp_fusion.2), kind=kCustom, calls=%fused_computation.clone.1 | custom fusion | bytes 7864352 | tf_op jit(solution)/shard_map/while/body/eval_jaxpr/jit(_take)/gather | solution.py:100
  189.6 4.4 %select_bitcast_fusion.2 = bf16[80,24,8,128]{3,1,0,2:T(8,128)(2,1)} fusion(bf16[8,80,24,128]{3,2,1,0:T(8,128)(2,1)} %gather_fusion, pred[8]{0:T(512)(128)(4,1)S(1)} %get-tuple-element.242), kind=kLoop, calls=%fused_computation.5.clone.1 | loop fusion | flops 1966080 | bytes 7864328 | tf_op jit(solution)/shard_map/while/body/eval_jaxpr/jit(_take)/select_n | solution.py:100
  195.6 4.1 %fusion.119 = f32[80,8,128]{2,0,1:T(8,128)S(1)} fusion(f32[24,8,128]{2,0,1:T(8,128)S(1)} %convert_bitcast_fusion.2, bf16[80,24,8,128]{3,1,0,2:T(8,128)(2,1)} %select_bitcast_fusion.2, s32[8,128]{1,0:T(8,128)S(1)} %get-tuple-element.244, s32[8,128]{1,0:T(8,128)S(1)} %get-tuple-element.245, s32[8,128]{1,0:T(8,128)S(1)} %get-tuple-element.246, ...), kind=kOutput, calls=%fused_computation.2.clone.1 | convolution fusion | flops 509263872 | bytes 4382720 | tf_op jit(solution)/shard_map/while/body/eval_jaxpr/kfjc,joc->kfjo/dot_general | solution.py:105
  199.9 5.1 %gather_fusion = bf16[8,80,24,128]{3,2,1,0:T(8,128)(2,1)} fusion(bf16[80,24,8,128]{3,1,2,0:T(8,128)(2,1)} %get-tuple-element.284, s32[1024]{0:T(1024)S(1)} %pad_clamp_fusion.2), kind=kCustom, calls=%fused_computation.clone.1 | custom fusion | bytes 7864352 | tf_op jit(solution)/shard_map/while/body/eval_jaxpr/jit(_take)/gather | solution.py:100
  205.0 4.4 %select_bitcast_fusion.2 = bf16[80,24,8,128]{3,1,0,2:T(8,128)(2,1)} fusion(bf16[8,80,24,128]{3,2,1,0:T(8,128)(2,1)} %gather_fusion, pred[8]{0:T(512)(128)(4,1)S(1)} %get-tuple-element.242), kind=kLoop, calls=%fused_computation.5.clone.1 | loop fusion | flops 1966080 | bytes 7864328 | tf_op jit(solution)/shard_map/while/body/eval_jaxpr/jit(_take)/select_n | solution.py:100
  215.2 5.1 %gather_fusion = bf16[8,80,24,128]{3,2,1,0:T(8,128)(2,1)} fusion(bf16[80,24,8,128]{3,1,2,0:T(8,128)(2,1)} %get-tuple-element.284, s32[1024]{0:T(1024)S(1)} %pad_clamp_fusion.2), kind=kCustom, calls=%fused_computation.clone.1 | custom fusion | bytes 7864352 | tf_op jit(solution)/shard_map/while/body/eval_jaxpr/jit(_take)/gather | solution.py:100
  220.3 4.4 %select_bitcast_fusion.2 = bf16[80,24,8,128]{3,1,0,2:T(8,128)(2,1)} fusion(bf16[8,80,24,128]{3,2,1,0:T(8,128)(2,1)} %gather_fusion, pred[8]{0:T(512)(128)(4,1)S(1)} %get-tuple-element.242), kind=kLoop, calls=%fused_computation.5.clone.1 | loop fusion | flops 1966080 | bytes 7864328 | tf_op jit(solution)/shard_map/while/body/eval_jaxpr/jit(_take)/select_n | solution.py:100
  234.0 4.7 %collective-permute-start.1 = (f32[1,80,81]{2,1,0:T(8,128)S(1)}, f32[1,80,81]{2,1,0:T(8,128)S(1)}, u32[]{:S(2)}, u32[]{:S(2)}) collective-permute-start(f32[1,80,81]{2,1,0:T(8,128)S(1)} %fusion.47), channel_id=1, source_target_pairs={{1,0},{2,1},{3,2},{4,3},{5,4},{6,5},{7,6},{0,7},{9,8},{10,9},{11,1... | collective-permute-start | bytes 77768 | tf_op jit(solution)/shard_map/ppermute | solution.py:20
  238.7 4.7 %convert_reduce_fusion = f32[24,8,128]{2,0,1:T(8,128)S(1)} fusion(bf16[80,24,8,128]{3,2,1,0:T(8,128)(2,1)} %bitcast.14), kind=kLoop, calls=%fused_computation.42 | loop fusion | flops 3907584 | bytes 4030464 | tf_op jit(solution)/shard_map/reduce_sum | solution.py:86
  246.3 4.8 %collective-permute-done.2 = f32[3,80,81]{2,1,0:T(8,128)S(1)} collective-permute-done((f32[3,80,81]{2,1,0:T(8,128)S(1)}, f32[3,80,81]{2,1,0:T(8,128)S(1)}, u32[]{:S(2)}, u32[]{:S(2)}) %collective-permute-start.2) | collective-permute-done | bytes 77792 | tf_op jit(solution)/shard_map/ppermute | solution.py:28
  261.7 7.8 %fusion.28 = bf16[80,24,8,128]{3,0,1,2:T(8,128)(2,1)S(1)} fusion(f32[24,8,128]{2,0,1:T(8,128)S(1)} %broadcast_multiply_fusion, bf16[80,24,8,128]{3,2,1,0:T(8,128)(2,1)} %bitcast.14, f32[8,80,80]{2,1,0:T(8,128)S(1)} %fusion.78, f32[8,80]{1,0:T(8,128)S(1)} %broadcast_divide_fusion, f32[8]{0:T(128)S(1)} %get-tuple-element.184), kind=kOutput, calls=%fused_computation.45 | convolution fusion | flops 324608000 | bytes 8170016 | tf_op jit(solution)/shard_map/kfbc,bkl->lfbc/dot_general | solution.py:136
  269.5 4.5 %copy.39 = bf16[80,24,8,128]{3,2,1,0:T(8,128)(2,1)} copy(bf16[80,24,8,128]{3,0,1,2:T(8,128)(2,1)S(1)} %fusion.28) | data formatting | bytes 7864320 | tf_op jit(solution)/shard_map/convert_element_type | solution.py:137
  (116 shorter events, 38.3 us)
Async XLA Ops:
  4.7 7.5 %copy-start = (bf16[1,1,64,4,128]{4,3,2,1,0:T(4,128)(2,1)S(1)}, bf16[1,1,64,4,128]{4,3,2,1,0:T(4,128)(2,1)}, u32[]{:S(2)}) copy-start(bf16[1,1,64,4,128]{4,3,2,1,0:T(4,128)(2,1)} %param.12) | copy-start | bytes 196612
  4.7 8.2 %copy-start.2 = (f32[1,1,64,128]{3,2,1,0:T(8,128)S(1)}, f32[1,1,64,128]{3,2,1,0:T(8,128)}, u32[]{:S(2)}) copy-start(f32[1,1,64,128]{3,2,1,0:T(8,128)} %param.16) | copy-start | bytes 98308
  4.7 97.5 %all-to-all-start = ((bf16[60,32,8,128]{3,2,0,1:T(8,128)(2,1)}), bf16[60,32,8,128]{3,2,0,1:T(8,128)(2,1)}, u32[]{:S(2)}, u32[]{:S(2)}) async-start(bf16[60,32,8,128]{3,2,0,1:T(8,128)(2,1)} %bitcast.137), calls=%async_computation | async-start | bytes 7864320 | tf_op jit(solution)/shard_map/all_to_all | solution.py:84
  102.2 5.4 %copy-start.3 = (s32[1,1,64]{2,1,0:T(1,128)S(1)}, s32[1,1,64]{2,1,0:T(1,128)}, u32[]{:S(2)}) copy-start(s32[1,1,64]{2,1,0:T(1,128)} %param.17) | copy-start | bytes 772
  230.5 0.8 copy-start.1
  233.9 17.5 %copy-start.4 = (s32[1,1,8,9]{3,2,1,0:T(8,128)S(1)}, s32[1,1,8,9]{3,2,1,0:T(8,128)}, u32[]{:S(2)}) copy-start(s32[1,1,8,9]{3,2,1,0:T(8,128)} %param.19) | copy-start | bytes 868
  233.9 9.5 %collective-permute-start = (f32[1,80,81]{2,1,0:T(8,128)S(1)}, f32[1,80,81]{2,1,0:T(8,128)S(1)}, u32[]{:S(2)}, u32[]{:S(2)}) collective-permute-start(f32[1,80,81]{2,1,0:T(8,128)S(1)} %fusion.47), channel_id=1, source_target_pairs={{0,1},{1,2},{2,3},{3,4},{4,5},{5,6},{6,7},{7,0},{8,9},{9,10},{10,1... | collective-permute-start | bytes 77768 | tf_op jit(solution)/shard_map/ppermute | solution.py:19
  234.0 9.4 %collective-permute-start.1 = (f32[1,80,81]{2,1,0:T(8,128)S(1)}, f32[1,80,81]{2,1,0:T(8,128)S(1)}, u32[]{:S(2)}, u32[]{:S(2)}) collective-permute-start(f32[1,80,81]{2,1,0:T(8,128)S(1)} %fusion.47), channel_id=1, source_target_pairs={{1,0},{2,1},{3,2},{4,3},{5,4},{6,5},{7,6},{0,7},{9,8},{10,9},{11,1... | collective-permute-start | bytes 77768 | tf_op jit(solution)/shard_map/ppermute | solution.py:20
  243.4 2.9 %collective-permute-start.3 = (f32[1,3,80,81]{3,2,1,0:T(8,128)S(1)}, f32[1,3,80,81]{3,2,1,0:T(8,128)S(1)}, u32[]{:S(2)}, u32[]{:S(2)}) collective-permute-start(f32[1,3,80,81]{3,2,1,0:T(8,128)S(1)} %get-tuple-element.183), channel_id=1, source_target_pairs={{0,8},{8,16},{16,24},{1,9},{9,17},{17,25},{2,10},{10,18},{18,26},{... | collective-permute-start | bytes 233288 | tf_op jit(solution)/shard_map/ppermute | solution.py:19
  244.7 6.4 %collective-permute-start.2 = (f32[3,80,81]{2,1,0:T(8,128)S(1)}, f32[3,80,81]{2,1,0:T(8,128)S(1)}, u32[]{:S(2)}, u32[]{:S(2)}) collective-permute-start(f32[3,80,81]{2,1,0:T(8,128)S(1)} %get-tuple-element.182), channel_id=1, source_target_pairs={{4,0},{5,1},{6,2},{7,3},{0,4},{1,5},{2,6},{3,7},{12,8},{13,9},{14,... | collective-permute-start | bytes 233288 | tf_op jit(solution)/shard_map/ppermute | solution.py:28
  244.8 6.3 %collective-permute-start.4 = (f32[1,3,80,81]{3,2,1,0:T(8,128)S(1)}, f32[1,3,80,81]{3,2,1,0:T(8,128)S(1)}, u32[]{:S(2)}, u32[]{:S(2)}) collective-permute-start(f32[1,3,80,81]{3,2,1,0:T(8,128)S(1)} %get-tuple-element.183), channel_id=1, source_target_pairs={{8,0},{16,8},{24,16},{9,1},{17,9},{25,17},{10,2},{18,10},{26,18},{... | collective-permute-start | bytes 233288 | tf_op jit(solution)/shard_map/ppermute | solution.py:20
where the time goes:
time: 277 us; the launch traced here: 274 us
  waiting for transfers between devices  94 us (34%)
  local copies, waits for them, and re-layouts  56.6 us (20%)
  other arithmetic  53.7 us (19%)
  matrix products  53.2 us (19%)
  starting transfers between devices  15 us (5%)
    all_to_all x1, waiting for transfers between devices, per_device(): lax.all_to_all(ordered, ('lat', 'lon'), split_axis=1, concat_axis=0, tile...  89.2 us
    gather x8, local copies, waits for them, and re-layouts, project_group(): picked = jnp.take(tile_state, group_rows, axis=2)  41 us
    select_n x8, other arithmetic, project_group(): picked = jnp.take(tile_state, group_rows, axis=2)  35.4 us
    dot_general x8, matrix products, project_group(): jnp.einsum('kfjc,joc->kfjo', picked, dense, preferred_element_type=jnp.fl...  33.1 us
    dot_general x1, matrix products, per_device(): jnp.einsum('kfbc,bkl->lfbc', deviation, transform, preferred_element_type...  7.83 us
    all_to_all x1, starting transfers between devices, per_device(): lax.all_to_all(ordered, ('lat', 'lon'), split_axis=1, concat_axis=0, tile...  7.44 us
    transpose x8, other arithmetic, project_group(): jnp.transpose(group_levels, (1, 0, 2))[None]  6.5 us
    ppermute x2, starting transfers between devices, padded(): after = lax.ppermute(leading, axis, down)  6.18 us
  transfers between devices with their start and end apart: 6, of which 2 were waited for; matrix products, arithmetic and copies ran while one was open for 2% of the time, Pallas kernels for 0%

commit v1 on v0

v1 whole, which is shorter than its diff:
```python
import functools
import math

import jax
import jax.numpy as jnp
from jax import lax
from jax.experimental import pallas as pl
from jax.experimental.pallas import tpu as pltpu
from jax.sharding import PartitionSpec as P

NS_ITERS = 6
MESH = pl.DeviceIdType.MESH
HIGHEST_PRECISION = lax.Precision.HIGHEST


def gather_kernel(
    plan,
    ens_ref,
    interp_ref,
    starts_ref,
    levels_ref,
    values_ref,
    weights_ref,
    rows_ref,
    count_ref,
    state_ref,
    slots_ref,
    dense,
    by_row,
    wide,
    obs,
    partial,
    send_sem,
    recv_sem,
    slot_send,
    slot_recv,
):
    lat_n, lon_n, share, tile_rows, tile_cols, levels_n, members, group = plan
    total = lat_n * lon_n
    halves = lon_n // group
    group_rows = group * share
    group_members = group_rows // levels_n
    padded_members = obs.shape[1] // (total // group)
    slots_n, stencil = interp_ref.shape[2:4]
    lat, lon = lax.axis_index("lat"), lax.axis_index("lon")
    me = lat * lon_n + lon
    half = lon // group

    barrier = pltpu.get_barrier_semaphore()

    @pl.loop(1, total)
    def _(step):
        peer = lax.rem(me + step, total)
        pl.semaphore_signal(
            barrier,
            inc=1,
            device_id={"lat": peer // lon_n, "lon": lax.rem(peer, lon_n)},
            device_id_type=MESH,
        )

    pl.semaphore_wait(barrier, total - 1)

    def tile_copy(to_lat, to_lon, source):
        return pltpu.make_async_remote_copy(
            src_ref=ens_ref.at[
                :,
                pl.ds(pl.multiple_of(to_lat * tile_rows, tile_rows), tile_rows),
                pl.ds(pl.multiple_of(to_lon * tile_cols, tile_cols), tile_cols),
            ],
            dst_ref=state_ref.at[pl.ds(source * share, share)],
            send_sem=send_sem.at[to_lat * lon_n + to_lon],
            recv_sem=recv_sem.at[source],
            device_id={"lat": to_lat, "lon": to_lon},
            device_id_type=MESH,
        )

    own = pltpu.make_async_copy(
        ens_ref.at[
            :,
            pl.ds(pl.multiple_of(lat * tile_rows, tile_rows), tile_rows),
            pl.ds(pl.multiple_of(lon * tile_cols, tile_cols), tile_cols),
        ],
        state_ref.at[pl.ds(me * share, share)],
        recv_sem.at[me],
    )
    own.start()
    reach = [u for u in range(1, halves)] + [0]

    @pl.loop(0, lat_n)
    def _(turn):
        to_lat = lax.rem(lat + lat_n - turn, lat_n)
        for u in reach:
            to_half = lax.rem(half + u, halves)

            @pl.loop(0, group)
            def _(i):
                to_lon = to_half * group + lax.rem(lon + i, group)

                @pl.when(to_lat * lon_n + to_lon != me)
                def _():
                    tile_copy(to_lat, to_lon, me).start()

    cells = lax.broadcasted_iota(jnp.int32, (tile_cols, starts_ref.shape[-1]), 0)

    @pl.loop(0, slots_n)
    def _(j):
        first = starts_ref[0, 0, pl.ds(j, 1), :]
        taps = interp_ref[0, 0, j].astype(jnp.float32)
        offset = cells - first
        grid = jnp.zeros(cells.shape, jnp.float32)
        for p in range(stencil):
            grid = jnp.where(offset == p, taps[p : p + 1, :], grid)
        dense[j] = grid.astype(jnp.bfloat16)

    def take_group(which):
        base = which * group_rows

        @pl.loop(0, group)
        def _(i):
            source = which * group + i
            tile_copy(source // lon_n, lax.rem(source, lon_n), source).wait_recv()

        @pl.loop(0, group_rows // 16)
        def _(i):
            piece = state_ref[pl.ds(base + i * 16, 16)].astype(jnp.float32)
            wide[pl.ds(pl.multiple_of(i * 16 * tile_rows, 16 * tile_rows), 16 * tile_rows), :] = (
                piece.reshape(16 * tile_rows, tile_cols)
            )

        for r in range(tile_rows):
            by_row[r] = wide[pl.ds(r, group_rows, stride=tile_rows), :].astype(jnp.bfloat16)

        @pl.loop(0, slots_n, unroll=4)
        def _(j):
            product = jnp.dot(by_row[rows_ref[j]], dense[j], preferred_element_type=jnp.float32)
            level = levels_ref[0, 0, j].astype(jnp.float32)
            folded = jnp.sum(
                product.reshape(group_members, levels_n, product.shape[1]) * level[None], axis=1
            )
            blank = jnp.zeros((padded_members - group_members, folded.shape[1]), jnp.float32)
            obs[j, pl.ds(pl.multiple_of(which * padded_members, 8), padded_members), :] = (
                jnp.concatenate([folded, blank], axis=0)
            )

    for u in range(halves):

        @pl.loop(0, lat_n)
        def _(turn):
            from_lat = lax.rem(lat + turn, lat_n)
            take_group(from_lat * halves + lax.rem(half + u, halves))

    span = obs.shape[1]
    row_ids = lax.broadcasted_iota(jnp.int32, (span, tile_cols), 0)
    real = lax.rem(row_ids, padded_members) < group_members

    def add_block(j, carry):
        block = obs[j]
        mean = jnp.sum(block, axis=0, keepdims=True) / members
        dev = jnp.where(real, block - mean, 0.0)
        innov = values_ref[0, 0, pl.ds(j, 1), :] - mean
        right = jnp.where(row_ids == group_members, innov, dev).astype(jnp.bfloat16)
        weight = weights_ref[0, 0, pl.ds(j, 1), :]
        live = jnp.where(jnp.full(weight.shape, j, jnp.int32) < count_ref[0], weight, 0.0)
        left = (dev * live).astype(jnp.bfloat16)
        return carry + lax.dot_general(
            left, right, (((1,), (1,)), ((), ())), preferred_element_type=jnp.float32
        )

    partial[...] = lax.fori_loop(
        0, slots_n, add_block, jnp.zeros((span, span), jnp.float32), unroll=4
    )

    def slot_copy(to_lat, to_lon, slot, out):
        return pltpu.make_async_remote_copy(
            src_ref=partial,
            dst_ref=slots_ref.at[slot],
            send_sem=slot_send.at[out],
            recv_sem=slot_recv.at[slot],
            device_id={"lat": to_lat, "lon": to_lon},
            device_id_type=MESH,
        )

    def away(distance):
        return lax.rem(lon + lon_n + distance, lon_n)

    last = lat_n - 1
    east_west = [slot_copy(lat, away(1), 3, 3), slot_copy(lat, away(-1), 5, 5)]
    south = [slot_copy(lat + 1, away(1 - s), s, s) for s in range(3)]
    north = [slot_copy(lat - 1, away(1 - s), 6 + s, 6 + s) for s in range(3)]
    pole = [slot_copy(lat, away(s - 1 - lon_n // 2), s, 6 + s) for s in range(3)]
    for copy in east_west:
        copy.start()

    @pl.when(lat < last)
    def _():
        for copy in south:
            copy.start()

    @pl.when(lat > 0)
    def _():
        for copy in north:
            copy.start()

    @pl.when(lat == 0)
    def _():
        for copy in pole:
            copy.start()

    slots_ref[4] = partial[...]

    @pl.when(lat == last)
    def _():
        for s in range(3):
            slots_ref[6 + s] = jnp.zeros((span, span), jnp.float32)

    @pl.loop(0, total)
    def _(peer):
        @pl.when(peer != me)
        def _():
            tile_copy(peer // lon_n, lax.rem(peer, lon_n), me).wait_send()

    for copy in east_west:
        copy.wait()
    for copy in pole:
        copy.wait_recv()
        copy.wait_send()

    @pl.when(lat < last)
    def _():
        for copy in south:
            copy.wait_send()
        for copy in north:
            copy.wait_recv()


def ensemble_transform(summed, members):
    identity = jnp.eye(members, dtype=jnp.float32)
    system = (members - 1) * identity + summed[:, :, :members]
    target = summed[:, :, members]
    scale = jnp.sqrt(jnp.sum(system * system, axis=(1, 2)))
    root_term = system / scale[:, None, None]
    inverse = jnp.broadcast_to(identity, system.shape)
    for repeat in range(NS_ITERS):
        middle = 1.5 * identity - 0.5 * jnp.einsum(
            "bij,bjk->bik", inverse, root_term, precision=HIGHEST_PRECISION
        )
        root_term = jnp.einsum("bij,bjk->bik", root_term, middle, precision=HIGHEST_PRECISION)
        inverse = jnp.einsum("bij,bjk->bik", middle, inverse, precision=HIGHEST_PRECISION)
    half_step = jnp.einsum("bij,bj->bi", inverse, target, precision=HIGHEST_PRECISION)
    shift_mean = (
        jnp.einsum("bij,bj->bi", inverse, half_step, precision=HIGHEST_PRECISION) / scale[:, None]
    )
    spread = jnp.sqrt(jnp.float32(members - 1)) * inverse / jnp.sqrt(scale)[:, None, None]
    return (spread + shift_mean[:, :, None]).astype(jnp.bfloat16)


def per_device(
    ensemble,
    obs_interp,
    obs_start,
    obs_levels,
    obs_values,
    obs_weight,
    obs_rows,
    obs_count,
    local_mask,
):
    lat_n = lax.axis_size("lat")
    lon_n = lax.axis_size("lon")
    total = lat_n * lon_n
    share, grid_rows, grid_cols = ensemble.shape
    tile_rows = grid_rows // lat_n
    tile_cols = grid_cols // lon_n
    slots_n, levels_n, obs_n = obs_levels.shape[2:]
    members = share * total // levels_n
    group = math.lcm(share, math.lcm(levels_n, 16)) // share
    groups = total // group
    group_members = group * share // levels_n
    padded_members = (group_members // 8 + 1) * 8
    span = groups * padded_members
    plan = (lat_n, lon_n, share, tile_rows, tile_cols, levels_n, members, group)
    vmem = pl.BlockSpec(memory_space=pltpu.VMEM)
    smem = pl.BlockSpec(memory_space=pltpu.SMEM)
    state, slots = pl.pallas_call(
        functools.partial(gather_kernel, plan),
        out_shape=(
            jax.ShapeDtypeStruct((share * total, tile_rows, tile_cols), jnp.bfloat16),
            jax.ShapeDtypeStruct((9, span, span), jnp.float32),
        ),
        in_specs=[pl.BlockSpec(memory_space=pl.ANY)] + [vmem] * 5 + [smem] * 2,
        out_specs=(vmem, vmem),
        scratch_shapes=[
            pltpu.VMEM((slots_n, tile_cols, obs_n), jnp.bfloat16),
            pltpu.VMEM((tile_rows, group * share, tile_cols), jnp.bfloat16),
            pltpu.VMEM((group * share * tile_rows, tile_cols), jnp.float32),
            pltpu.VMEM((slots_n, span, obs_n), jnp.float32),
            pltpu.VMEM((span, span), jnp.float32),
            pltpu.SemaphoreType.DMA((total,)),
            pltpu.SemaphoreType.DMA((total,)),
            pltpu.SemaphoreType.DMA((9,)),
            pltpu.SemaphoreType.DMA((9,)),
        ],
        compiler_params=pltpu.CompilerParams(
            collective_id=0, has_side_effects=True, vmem_limit_bytes=40 * 1024 * 1024
        ),
    )(
        ensemble,
        obs_interp,
        obs_start,
        obs_levels,
        obs_values,
        obs_weight,
        obs_rows.reshape(-1),
        obs_count.reshape(-1),
    )
    tile_state = state.reshape(members, levels_n, tile_rows, tile_cols)
    ens_mean = jnp.sum(tile_state, axis=0, dtype=jnp.float32) / members
    deviation = (tile_state - ens_mean).astype(jnp.bfloat16)
    slot_mask = local_mask[0, 0].astype(jnp.float32)
    spread = jnp.dot(slot_mask, slots.reshape(9, span * span), precision=HIGHEST_PRECISION)
    spread = spread.reshape(tile_rows, groups, padded_members, groups, padded_members)
    system = spread[:, :, :group_members, :, :group_members].reshape(tile_rows, members, members)
    target = spread[:, :, :group_members, 0, group_members].reshape(tile_rows, members, 1)
    transform = ensemble_transform(jnp.concatenate([system, target], axis=2), members)
    update = jnp.einsum("kfbc,bkl->lfbc", deviation, transform, preferred_element_type=jnp.float32)
    return (ens_mean[None] + update).astype(jnp.bfloat16)


def solution(mesh):
    placed = (
        P(("lat", "lon"), None, None),
        P("lat", "lon", None, None, None),
        P("lat", "lon", None, None),
        P("lat", "lon", None, None, None),
        P("lat", "lon", None, None),
        P("lat", "lon", None, None),
        P("lat", "lon", None),
        P("lat", "lon"),
        P("lat", "lon", None, None),
    )
    return jax.shard_map(
        per_device,
        mesh=mesh,
        in_specs=placed,
        out_specs=P(None, None, "lat", "lon"),
        check_vma=False,
    )
```

time: 277 us -> 155 us (0.56)
  Pallas kernels: 0 us -> 112 us
  waiting for transfers between devices: 94 us -> 0 us
  other arithmetic: 53.7 us -> 4.23 us
  matrix products: 53.2 us -> 15.4 us
  local copies, waits for them, and re-layouts: 56.6 us -> 21.5 us
  starting transfers between devices: 15 us -> 0 us
    pallas_call x0 -> x1, Pallas kernels: none -> 112 us  [per_device(): pl.pallas_call(functools.partial(gather_kernel, plan), out_shape=(jax.Sha...]
    all_to_all x1 -> x0, waiting for transfers between devices: 89.2 us -> none  [per_device(): lax.all_to_all(ordered, ('lat', 'lon'), split_axis=1, concat_axis=0, tile...]
    gather x8 -> x0, local copies, waits for them, and re-layouts: 41 us -> none  [project_group(): picked = jnp.take(tile_state, group_rows, axis=2)]
    select_n x9 -> x0, other arithmetic: 35.5 us -> none  [the longest x8 35.4 us: project_group(): picked = jnp.take(tile_state, group_rows, axis=2)]
    dot_general x10 -> x1, matrix products: 36.1 us -> 0.72 us  [per_device(): jnp.dot(slot_mask, slots.reshape(9, span * span), precision=HIGHEST_PRECI...]
    unnamed x11 -> x22, local copies, waits for them, and re-layouts: 0.28 us -> 9.48 us
    ppermute x5 -> x0, starting transfers between devices: 7.61 us -> none  [the longest x2 6.18 us: padded(): after = lax.ppermute(leading, axis, down)]
    all_to_all x1 -> x0, starting transfers between devices: 7.44 us -> none  [per_device(): lax.all_to_all(ordered, ('lat', 'lon'), split_axis=1, concat_axis=0, tile...]
  transfers between devices with their start and end apart: 6 -> 0, of which waited for: 2 -> 0; matrix products, arithmetic and copies ran while one was open for 2% -> 0% of each run, Pallas kernels for 0% -> 0%
where the time goes in v1:
time: 155 us; the launch traced here: 154 us
  Pallas kernels  112 us (72%)
  local copies, waits for them, and re-layouts  21.5 us (14%)
  matrix products  15.4 us (10%)
  other arithmetic  4.23 us (3%)
    pallas_call x1, Pallas kernels, per_device(): pl.pallas_call(functools.partial(gather_kernel, plan), out_shape=(jax.Sha...  112 us
    unnamed x22, local copies, waits for them, and re-layouts  9.48 us
    dot_general x1, matrix products, per_device(): jnp.einsum('kfbc,bkl->lfbc', deviation, transform, preferred_element_type...  5.37 us
    convert_element_type x1, local copies, waits for them, and re-layouts, per_device(): return (ens_mean[None] + update).astype(jnp.bfloat16)  4.45 us
    slice x1, local copies, waits for them, and re-layouts, per_device(): spread[:, :, :group_members, 0, group_members]  3.45 us
    reshape x1, local copies, waits for them, and re-layouts, per_device(): spread.reshape(tile_rows, groups, padded_members, groups, padded_members)  3.34 us

profile of v1, /device:TPU:0, one launch (start us, length us, event | category | flops | bytes accessed | tf_op | source)
XLA Modules:
  0.0 154.5 jit_solution(10939379863941971867)
XLA Ops:
  0.9 2.1 %copy-done.2 = bf16[60,32,1024]{2,1,0:T(8,128)(2,1)S(1)} copy-done((bf16[60,32,1024]{2,1,0:T(8,128)(2,1)S(1)}, bf16[60,32,1024]{2,1,0:T(8,128)(2,1)}, u32[]{:S(2)}) %copy-start.2) | copy-done | bytes 3932184
  3.0 1.0 copy-done.3
  4.0 0.8 copy-done.4
  4.8 0.8 copy-done.5
  5.6 0.8 copy-done.6
  6.3 0.8 copy-done.7
  7.1 0.7 copy-done.8
  7.7 112.4 %shard_map.91 = (bf16[1920,8,128]{2,1,0:T(8,128)(2,1)S(1)}, f32[9,128,128]{2,1,0:T(8,128)S(1)}) custom-call(bf16[60,32,1024]{2,1,0:T(8,128)(2,1)S(1)} %copy-done.2, bf16[1,1,64,4,128]{4,3,2,1,0:T(4,128)(2,1)S(1)} %copy-done.4, s32[1,1,64,128]{3,2,1,0:T(8,128)S(1)} %copy-done.5, bf16[1,1,64,24,128]{4,3,2,1,0:T(8,128)(2,1)S(1)} %copy-done.3, ...), custom_call_target="tpu_custom_call" | custom-call | tf_op jit(solution)/shard_map/pallas_call | solution.py:284
  120.1 1.9 %copy-done = bf16[1920,8,128]{2,1,0:T(8,128)(2,1)} copy-done((bf16[1920,8,128]{2,1,0:T(8,128)(2,1)}, bf16[1920,8,128]{2,1,0:T(8,128)(2,1)S(1)}, u32[]{:S(2)}) %copy-start) | copy-done | bytes 3932184
  122.1 0.6 convert_reduce_fusion
  122.8 0.6 copy.30
  123.4 0.7 convolution_bitcast_fusion
  124.1 3.3 %reshape.52 = f32[8,8,16,8,16]{4,3,2,1,0:T(8,128)} reshape(f32[8,16384]{1,0:T(8,128)S(1)} %convolution_bitcast_fusion) | data formatting | bytes 1048576 | tf_op jit(solution)/shard_map/reshape | solution.py:321
  127.5 3.4 %slice_reduce_fusion = f32[8,8,10]{2,1,0:T(8,128)S(1)} fusion(f32[8,8,16,8,16]{4,3,2,1,0:T(8,128)} %reshape.52), kind=kLoop, calls=%fused_computation.22 | loop fusion | bytes 5120 | tf_op jit(solution)/shard_map/slice | solution.py:323
  130.9 2.3 %multiply_reduce_fusion = (f32[8]{0:T(128)S(1)}, f32[8,8,10,8,10]{4,3,2,1,0:T(8,128)S(1)}) fusion(f32[8,10,8,10]{3,2,1,0:T(8,128)S(1)} %compare_select_fusion, f32[8,8,16,8,16]{4,3,2,1,0:T(8,128)} %reshape.52), kind=kLoop, calls=%fused_computation.7 | loop fusion | flops 153592 | bytes 435232 | tf_op jit(solution)/shard_map/reduce_sum | solution.py:240
  133.3 0.7 reshape.53
  134.0 0.5 fusion.7
  134.5 0.5 fusion.22
  135.5 0.5 fusion.8
  135.9 0.5 fusion.27
  136.4 0.5 fusion.26
  136.9 0.5 fusion.9
  137.4 0.5 fusion.29
  138.3 0.5 fusion.10
  139.7 0.5 fusion.11
  140.2 0.6 fusion.32
  141.3 0.5 fusion.12
  142.2 0.6 convolution_bitcast_fusion.1
  142.8 0.6 fusion.35
  143.6 1.1 convert.1
  144.6 5.4 %fusion = bf16[80,24,8,128]{3,0,1,2:T(8,128)(2,1)S(1)} fusion(f32[24,8,128]{2,0,1:T(8,128)S(1)} %copy.17, f32[80,24,8,128]{3,2,1,0:T(8,128)S(1)} %convert.1, f32[8,80,80]{2,1,0:T(8,128)S(1)} %fusion.34, f32[8,80]{1,0:T(8,128)S(1)} %broadcast_divide_fusion, f32[8]{0:T(128)S(1)} %get-tuple-element.11), kind=kOutput, calls=%fused_computation.2 | convolution fusion | flops 322641920 | bytes 12102176 | tf_op jit(solution)/shard_map/kfbc,bkl->lfbc/dot_general | solution.py:325
  150.0 4.5 %copy.21 = bf16[80,24,8,128]{3,2,1,0:T(8,128)(2,1)} copy(bf16[80,24,8,128]{3,0,1,2:T(8,128)(2,1)S(1)} %fusion) | data formatting | bytes 7864320 | tf_op jit(solution)/shard_map/convert_element_type | solution.py:326
  (28 shorter events, 3.2 us)
Async XLA Ops:
  0.9 2.1 %copy-start.2 = (bf16[60,32,1024]{2,1,0:T(8,128)(2,1)S(1)}, bf16[60,32,1024]{2,1,0:T(8,128)(2,1)}, u32[]{:S(2)}) copy-start(bf16[60,32,1024]{2,1,0:T(8,128)(2,1)} %ens_ref.1) | copy-start | bytes 11796484
  3.0 1.0 copy-start.3
  4.0 0.8 copy-start.4
  4.8 0.8 copy-start.5
  5.6 0.8 copy-start.6
  6.3 0.8 copy-start.7
  7.1 0.7 copy-start.8
  120.1 1.9 %copy-start = (bf16[1920,8,128]{2,1,0:T(8,128)(2,1)}, bf16[1920,8,128]{2,1,0:T(8,128)(2,1)S(1)}, u32[]{:S(2)}) copy-start(bf16[1920,8,128]{2,1,0:T(8,128)(2,1)S(1)} %get-tuple-element.7) | copy-start | bytes 11796484
  120.1 3.2 %copy-start.9 = (s32[1,1,8,9]{3,2,1,0:T(8,128)S(1)}, s32[1,1,8,9]{3,2,1,0:T(8,128)}, u32[]{:S(2)}) copy-start(s32[1,1,8,9]{3,2,1,0:T(8,128)} %param.17) | copy-start | bytes 868
  138.3 5.3 %copy-start.1 = (bf16[1920,8,128]{2,1,0:T(8,128)(2,1)S(1)}, bf16[1920,8,128]{2,1,0:T(8,128)(2,1)}, u32[]{:S(2)}) copy-start(bf16[1920,8,128]{2,1,0:T(8,128)(2,1)} %copy-done) | copy-start | bytes 11796484

commit v2 on v1

--- a/solution.py
+++ b/solution.py
@@ -10,21 +10,25 @@
 
 NS_ITERS = 6
 MESH = pl.DeviceIdType.MESH
-HIGHEST_PRECISION = lax.Precision.HIGHEST
 
 
 def gather_kernel(
     plan,
     ens_ref,
+    interp_in,
+    starts_in,
+    levels_in,
+    values_in,
+    weights_in,
+    rows_ref,
+    count_ref,
+    state_ref,
+    slots_ref,
     interp_ref,
     starts_ref,
     levels_ref,
     values_ref,
     weights_ref,
-    rows_ref,
-    count_ref,
-    state_ref,
-    slots_ref,
     dense,
     by_row,
     wide,
@@ -34,6 +38,7 @@
     recv_sem,
     slot_send,
     slot_recv,
+    load_sem,
 ):
     lat_n, lon_n, share, tile_rows, tile_cols, levels_n, members, group = plan
     total = lat_n * lon_n
@@ -100,6 +105,23 @@
                 def _():
                     tile_copy(to_lat, to_lon, me).start()
 
+    loads = [
+        pltpu.make_async_copy(source, target, load_sem.at[i])
+        for i, (source, target) in enumerate(
+            [
+                (interp_in, interp_ref),
+                (starts_in, starts_ref),
+                (levels_in, levels_ref),
+                (values_in, values_ref),
+                (weights_in, weights_ref),
+            ]
+        )
+    ]
+    for copy in loads:
+        copy.start()
+    for copy in loads:
+        copy.wait()
+
     cells = lax.broadcasted_iota(jnp.int32, (tile_cols, starts_ref.shape[-1]), 0)
 
     @pl.loop(0, slots_n)
@@ -233,25 +255,141 @@
             copy.wait_recv()
 
 
-def ensemble_transform(summed, members):
-    identity = jnp.eye(members, dtype=jnp.float32)
-    system = (members - 1) * identity + summed[:, :, :members]
-    target = summed[:, :, members]
-    scale = jnp.sqrt(jnp.sum(system * system, axis=(1, 2)))
-    root_term = system / scale[:, None, None]
-    inverse = jnp.broadcast_to(identity, system.shape)
-    for repeat in range(NS_ITERS):
-        middle = 1.5 * identity - 0.5 * jnp.einsum(
-            "bij,bjk->bik", inverse, root_term, precision=HIGHEST_PRECISION
-        )
-        root_term = jnp.einsum("bij,bjk->bik", root_term, middle, precision=HIGHEST_PRECISION)
-        inverse = jnp.einsum("bij,bjk->bik", middle, inverse, precision=HIGHEST_PRECISION)
-    half_step = jnp.einsum("bij,bj->bi", inverse, target, precision=HIGHEST_PRECISION)
-    shift_mean = (
-        jnp.einsum("bij,bj->bi", inverse, half_step, precision=HIGHEST_PRECISION) / scale[:, None]
-    )
-    spread = jnp.sqrt(jnp.float32(members - 1)) * inverse / jnp.sqrt(scale)[:, None, None]
-    return (spread + shift_mean[:, :, None]).astype(jnp.bfloat16)
+def split_dot(left, right):
+    left_high = left.astype(jnp.bfloat16)
+    left_low = (left - left_high.astype(jnp.float32)).astype(jnp.bfloat16)
+    right_high = right.astype(jnp.bfloat16)
+    right_low = (right - right_high.astype(jnp.float32)).astype(jnp.bfloat16)
+    return jnp.dot(
+        jnp.concatenate([left_high, left_high, left_low], axis=1),
+        jnp.concatenate([right_high, right_low, right_high], axis=0),
+        preferred_element_type=jnp.float32,
+    )
+
+
+def analysis_kernel(
+    plan,
+    state_ref,
+    slots_ref,
+    mask_ref,
+    out_ref,
+    root,
+    inverse,
+    target,
+    scales,
+    wide,
+    big,
+    dev,
+    mean,
+    result,
+    out_sem,
+):
+    members, levels_n, tile_rows, tile_cols, group_members, padded_members, ns_iters = plan
+    span = slots_ref.shape[1]
+    deep = members * tile_rows
+    rows = lax.broadcasted_iota(jnp.int32, (span, span), 0)
+    cols = lax.broadcasted_iota(jnp.int32, (span, span), 1)
+    real_cols = lax.rem(cols, padded_members) < group_members
+    identity = jnp.where((rows == cols) & real_cols, 1.0, 0.0)
+
+    @pl.loop(0, tile_rows)
+    def _(b):
+        summed = mask_ref[b * 9].astype(jnp.float32) * slots_ref[0]
+        for slot in range(1, 9):
+            summed += mask_ref[b * 9 + slot].astype(jnp.float32) * slots_ref[slot]
+        system = (members - 1) * identity + jnp.where(real_cols, summed, 0.0)
+        total = jnp.sum(jnp.sum(system * system, axis=0, keepdims=True), axis=1, keepdims=True)
+        scale = jnp.sqrt(total)
+        scales[b] = jnp.broadcast_to(scale, scales.shape[1:])
+        target[b] = jnp.sum(
+            jnp.where(cols == group_members, summed, 0.0), axis=1, keepdims=True
+        )
+        root_term = system / scale
+        middle = 1.5 * identity - 0.5 * root_term
+        root[b] = split_dot(root_term, middle)
+        inverse[b] = middle
+
+    @pl.loop(0, levels_n)
+    def _(f):
+        cell = state_ref[:, f].astype(jnp.float32)
+        average = jnp.sum(cell, axis=0) / members
+        mean[f] = average
+        dev[f] = (cell - average[None]).reshape(deep, tile_cols).astype(jnp.bfloat16)
+
+    @pl.loop(0, ns_iters - 2)
+    def _(repeat):
+        for b in range(tile_rows):
+            root_term, term = root[b], inverse[b]
+            middle = 1.5 * identity - 0.5 * split_dot(term, root_term)
+            root[b] = split_dot(root_term, middle)
+            inverse[b] = split_dot(middle, term)
+
+    chosen = lax.broadcasted_iota(jnp.int32, (members, span), 0)
+    place = lax.broadcasted_iota(jnp.int32, (members, span), 1)
+    picked = (place // padded_members) * group_members + lax.rem(place, padded_members)
+    pick = jnp.where(
+        (picked == chosen) & (lax.rem(place, padded_members) < group_members), 1.0, 0.0
+    ).astype(jnp.bfloat16)
+    source = lax.broadcasted_iota(jnp.int32, (span, deep), 0)
+    spot = lax.broadcasted_iota(jnp.int32, (span, deep), 1)
+    member_of = (source // padded_members) * group_members + lax.rem(source, padded_members)
+    spot = jnp.where(
+        lax.rem(source, padded_members) < group_members, spot - member_of * tile_rows, -1
+    )
+
+    for b in range(tile_rows):
+        term = inverse[b]
+        middle = 1.5 * identity - 0.5 * split_dot(term, root[b])
+        term = split_dot(middle, term)
+        scale = scales[b][:1, :1]
+        half_step = jnp.sum(term * target[b], axis=0, keepdims=True)
+        shift = jnp.sum(term * half_step, axis=1, keepdims=True) / scale
+        spread = jnp.sqrt(jnp.float32(members - 1)) * term / jnp.sqrt(scale)
+        transform = (spread + shift).astype(jnp.bfloat16)
+        turned = lax.dot_general(
+            pick, transform, (((1,), (1,)), ((), ())), preferred_element_type=jnp.float32
+        ).astype(jnp.bfloat16)
+        spread_out = jnp.dot(
+            turned,
+            jnp.where(spot == b, 1.0, 0.0).astype(jnp.bfloat16),
+            preferred_element_type=jnp.float32,
+        )
+        for part in range(deep // tile_cols):
+            wide[part, pl.ds(b, members, stride=tile_rows), :] = spread_out[
+                :, part * tile_cols : (part + 1) * tile_cols
+            ]
+
+    for part in range(deep // tile_cols):
+        big[:, part * tile_cols : (part + 1) * tile_cols] = wide[part].astype(jnp.bfloat16)
+
+    def send(pair):
+        return pltpu.make_async_copy(
+            result.at[:, pl.ds(pair * 2, 2)], out_ref.at[:, pl.ds(pair * 2, 2)], out_sem.at[pair]
+        )
+
+    chunk = 128
+
+    @pl.loop(0, levels_n // 2)
+    def _(pair):
+        f = pair * 2
+        right = jnp.concatenate([dev[f], dev[f + 1]], axis=1)
+        averages = [mean[f], mean[f + 1]]
+        for first in range(0, deep, chunk):
+            update = jnp.dot(
+                big[first : first + chunk, :], right, preferred_element_type=jnp.float32
+            )
+            for half in range(2):
+                block = update[:, half * tile_cols : (half + 1) * tile_cols].reshape(
+                    chunk // tile_rows, tile_rows, tile_cols
+                )
+                result[first // tile_rows : (first + chunk) // tile_rows, f + half] = (
+                    block + averages[half][None]
+                ).astype(jnp.bfloat16)
+        send(pair).start()
+
+    @pl.loop(0, levels_n // 2)
+    def _(pair):
+        send(pair).wait()
 
 
 def per_device(
@@ -287,9 +425,13 @@
             jax.ShapeDtypeStruct((share * total, tile_rows, tile_cols), jnp.bfloat16),
             jax.ShapeDtypeStruct((9, span, span), jnp.float32),
         ),
-        in_specs=[pl.BlockSpec(memory_space=pl.ANY)] + [vmem] * 5 + [smem] * 2,
+        in_specs=[pl.BlockSpec(memory_space=pltpu.HBM)] * 6 + [smem] * 2,
         out_specs=(vmem, vmem),
         scratch_shapes=[
+            pltpu.VMEM(array.shape, array.dtype)
+            for array in (obs_interp, obs_start, obs_levels, obs_values, obs_weight)
+        ]
+        + [
             pltpu.VMEM((slots_n, tile_cols, obs_n), jnp.bfloat16),
             pltpu.VMEM((tile_rows, group * share, tile_cols), jnp.bfloat16),
             pltpu.VMEM((group * share * tile_rows, tile_cols), jnp.float32),
@@ -299,9 +441,10 @@
             pltpu.SemaphoreType.DMA((total,)),
             pltpu.SemaphoreType.DMA((9,)),
             pltpu.SemaphoreType.DMA((9,)),
+            pltpu.SemaphoreType.DMA((5,)),
         ],
         compiler_params=pltpu.CompilerParams(
-            collective_id=0, has_side_effects=True, vmem_limit_bytes=40 * 1024 * 1024
+            collective_id=0, has_side_effects=True, vmem_limit_bytes=54 * 1024 * 1024
         ),
     )(
         ensemble,
@@ -314,16 +457,28 @@
         obs_count.reshape(-1),
     )
     tile_state = state.reshape(members, levels_n, tile_rows, tile_cols)
-    ens_mean = jnp.sum(tile_state, axis=0, dtype=jnp.float32) / members
-    deviation = (tile_state - ens_mean).astype(jnp.bfloat16)
-    slot_mask = local_mask[0, 0].astype(jnp.float32)
-    spread = jnp.dot(slot_mask, slots.reshape(9, span * span), precision=HIGHEST_PRECISION)
-    spread = spread.reshape(tile_rows, groups, padded_members, groups, padded_members)
-    system = spread[:, :, :group_members, :, :group_members].reshape(tile_rows, members, members)
-    target = spread[:, :, :group_members, 0, group_members].reshape(tile_rows, members, 1)
-    transform = ensemble_transform(jnp.concatenate([system, target], axis=2), members)
-    update = jnp.einsum("kfbc,bkl->lfbc", deviation, transform, preferred_element_type=jnp.float32)
-    return (ens_mean[None] + update).astype(jnp.bfloat16)
+    tiles = (tile_rows, span, span)
+    deep = members * tile_rows
+    plan = (members, levels_n, tile_rows, tile_cols, group_members, padded_members, NS_ITERS)
+    return pl.pallas_call(
+        functools.partial(analysis_kernel, plan),
+        out_shape=jax.ShapeDtypeStruct(tile_state.shape, jnp.bfloat16),
+        in_specs=[vmem, vmem, smem],
+        out_specs=pl.BlockSpec(memory_space=pltpu.HBM),
+        scratch_shapes=[
+            pltpu.VMEM(tiles, jnp.float32),
+            pltpu.VMEM(tiles, jnp.float32),
+            pltpu.VMEM((tile_rows, span, 1), jnp.float32),
+            pltpu.VMEM((tile_rows, 8, 128), jnp.float32),
+            pltpu.VMEM((deep // tile_cols, deep, tile_cols), jnp.float32),
+            pltpu.VMEM((deep, deep), jnp.bfloat16),
+            pltpu.VMEM((levels_n, deep, tile_cols), jnp.bfloat16),
+            pltpu.VMEM((levels_n, tile_rows, tile_cols), jnp.float32),
+            pltpu.VMEM(tile_state.shape, jnp.bfloat16),
+            pltpu.SemaphoreType.DMA((levels_n // 2,)),
+        ],
+        compiler_params=pltpu.CompilerParams(vmem_limit_bytes=40 * 1024 * 1024),
+    )(tile_state, slots, local_mask.reshape(-1))
 
 
 def solution(mesh):

time: 155 us -> 146 us (0.942)
  Pallas kernels: 112 us -> 141 us
  local copies, waits for them, and re-layouts: 21.5 us -> 3.94 us
  matrix products: 15.4 us -> 0 us
  other arithmetic: 4.23 us -> 0 us
    pallas_call x0 -> x1, Pallas kernels: none -> 25.2 us  [per_device(): pl.pallas_call(functools.partial(analysis_kernel, plan), out_shape=jax.Sh...]
    dot_general x21 -> x0, matrix products: 15.4 us -> none  [the longest x1 5.37 us: per_device(): jnp.einsum('kfbc,bkl->lfbc', deviation, transform, preferred_element_type...]
    unnamed x22 -> x4, local copies, waits for them, and re-layouts: 9.48 us -> 3.17 us
    convert_element_type x1 -> x0, local copies, waits for them, and re-layouts: 4.45 us -> none  [per_device(): return (ens_mean[None] + update).astype(jnp.bfloat16)]
    pallas_call x1, Pallas kernels: 112 us -> 116 us  [per_device(): pl.pallas_call(functools.partial(gather_kernel, plan), out_shape=(jax.Sha...]
    slice x1 -> x0, local copies, waits for them, and re-layouts: 3.45 us -> none  [per_device(): spread[:, :, :group_members, 0, group_members]]
    reshape x2 -> x1, local copies, waits for them, and re-layouts: 4.02 us -> 0.77 us  [per_device(): local_mask.reshape(-1)]
    reduce_sum x2 -> x0, other arithmetic: 2.91 us -> none  [the longest x1 2.33 us: ensemble_transform(): scale = jnp.sqrt(jnp.sum(system * system, axis=(1, 2)))]
where the time goes in v2:
time: 146 us
  Pallas kernels  141 us (97%)
  local copies, waits for them, and re-layouts  3.94 us (3%)
    pallas_call x1, Pallas kernels, per_device(): pl.pallas_call(functools.partial(gather_kernel, plan), out_shape=(jax.Sha...  116 us
    pallas_call x1, Pallas kernels, per_device(): pl.pallas_call(functools.partial(analysis_kernel, plan), out_shape=jax.Sh...  25.2 us
    unnamed x4, local copies, waits for them, and re-layouts  3.17 us

profile of v2, /device:TPU:0, one launch (start us, length us, event | category | flops | bytes accessed | tf_op | source)
XLA Modules:
  0.0 146.0 jit_solution(17842344086833634676)
XLA Ops:
  0.7 0.8 reshape.15.mask_ref
  1.4 116.2 %shard_map.91 = (bf16[1920,8,128]{2,1,0:T(8,128)(2,1)}, f32[9,128,128]{2,1,0:T(8,128)}) custom-call(bf16[60,32,1024]{2,1,0:T(8,128)(2,1)} %ens_ref.1, bf16[1,1,64,4,128]{4,3,2,1,0:T(4,128)(2,1)} %interp_in.1, s32[1,1,64,128]{3,2,1,0:T(8,128)} %starts_in.1, bf16[1,1,64,24,128]{4,3,2,1,0:T(8,128)(2,1)} %levels_in.1, f32[1,1,64,128]{3,2,1,0:T(8,128)} %values_in.1, ...), custom_call_target="tpu_custom_call" | custom-call | tf_op jit(solution)/shard_map/pallas_call | solution.py:422
  117.6 0.0 copy-start
  117.6 2.1 %copy-done = bf16[1920,8,128]{2,1,0:T(8,128)(2,1)S(1)} copy-done((bf16[1920,8,128]{2,1,0:T(8,128)(2,1)S(1)}, bf16[1920,8,128]{2,1,0:T(8,128)(2,1)}, u32[]{:S(2)}) %copy-start) | copy-done | bytes 3932184
  119.7 0.0 copy-start.1
  119.7 1.1 copy-done.1
  120.8 25.2 %shard_map.92 = bf16[80,24,8,128]{3,2,1,0:T(8,128)(2,1)} custom-call(bf16[80,24,8,128]{3,2,1,0:T(8,128)(2,1)S(1)} %bitcast.6, f32[9,128,128]{2,1,0:T(8,128)S(1)} %copy-done.1, s32[72]{0:T(128)S(1)} %reshape.15.mask_ref), custom_call_target="tpu_custom_call" | custom-call | tf_op jit(solution)/shard_map/pallas_call | solution.py:463
Async XLA Ops:
  117.6 2.1 %copy-start = (bf16[1920,8,128]{2,1,0:T(8,128)(2,1)S(1)}, bf16[1920,8,128]{2,1,0:T(8,128)(2,1)}, u32[]{:S(2)}) copy-start(bf16[1920,8,128]{2,1,0:T(8,128)(2,1)} %get-tuple-element.7) | copy-start | bytes 11796484
  119.7 1.1 copy-start.1

commit v3 on v2

--- a/solution.py
+++ b/solution.py
@@ -292,7 +292,7 @@
     real_cols = lax.rem(cols, padded_members) < group_members
     identity = jnp.where((rows == cols) & real_cols, 1.0, 0.0)
 
-    @pl.loop(0, tile_rows)
+    @pl.loop(0, tile_rows, unroll=4)
     def _(b):
         summed = mask_ref[b * 9].astype(jnp.float32) * slots_ref[0]
         for slot in range(1, 9):
@@ -309,7 +309,7 @@
         root[b] = split_dot(root_term, middle)
         inverse[b] = middle
 
-    @pl.loop(0, levels_n)
+    @pl.loop(0, levels_n, unroll=2)
     def _(f):
         cell = state_ref[:, f].astype(jnp.float32)
         average = jnp.sum(cell, axis=0) / members

time: 146 us -> 144 us (0.986)
  Pallas kernels: 141 us -> 139 us
    pallas_call x1, Pallas kernels: 25.2 us -> 22.6 us  [per_device(): pl.pallas_call(functools.partial(analysis_kernel, plan), out_shape=jax.Sh...]
where the time goes in v3:
time: 144 us; the launch traced here: 143 us
  Pallas kernels  139 us (97%)
  local copies, waits for them, and re-layouts  3.94 us (3%)
    pallas_call x1, Pallas kernels, per_device(): pl.pallas_call(functools.partial(gather_kernel, plan), out_shape=(jax.Sha...  116 us
    pallas_call x1, Pallas kernels, per_device(): pl.pallas_call(functools.partial(analysis_kernel, plan), out_shape=jax.Sh...  22.6 us
    unnamed x4, local copies, waits for them, and re-layouts  3.17 us

profile of v3, /device:TPU:0, one launch (start us, length us, event | category | flops | bytes accessed | tf_op | source)
XLA Modules:
  0.0 143.4 jit_solution(2714363830109772720)
XLA Ops:
  0.7 0.8 reshape.15.mask_ref
  1.4 116.2 %shard_map.91 = (bf16[1920,8,128]{2,1,0:T(8,128)(2,1)}, f32[9,128,128]{2,1,0:T(8,128)}) custom-call(bf16[60,32,1024]{2,1,0:T(8,128)(2,1)} %ens_ref.1, bf16[1,1,64,4,128]{4,3,2,1,0:T(4,128)(2,1)} %interp_in.1, s32[1,1,64,128]{3,2,1,0:T(8,128)} %starts_in.1, bf16[1,1,64,24,128]{4,3,2,1,0:T(8,128)(2,1)} %levels_in.1, f32[1,1,64,128]{3,2,1,0:T(8,128)} %values_in.1, ...), custom_call_target="tpu_custom_call" | custom-call | tf_op jit(solution)/shard_map/pallas_call | solution.py:422
  117.6 0.0 copy-start
  117.6 2.1 %copy-done = bf16[1920,8,128]{2,1,0:T(8,128)(2,1)S(1)} copy-done((bf16[1920,8,128]{2,1,0:T(8,128)(2,1)S(1)}, bf16[1920,8,128]{2,1,0:T(8,128)(2,1)}, u32[]{:S(2)}) %copy-start) | copy-done | bytes 3932184
  119.7 0.0 copy-start.1
  119.7 1.1 copy-done.1
  120.8 22.6 %shard_map.92 = bf16[80,24,8,128]{3,2,1,0:T(8,128)(2,1)} custom-call(bf16[80,24,8,128]{3,2,1,0:T(8,128)(2,1)S(1)} %bitcast.6, f32[9,128,128]{2,1,0:T(8,128)S(1)} %copy-done.1, s32[72]{0:T(128)S(1)} %reshape.15.mask_ref), custom_call_target="tpu_custom_call" | custom-call | tf_op jit(solution)/shard_map/pallas_call | solution.py:463
Async XLA Ops:
  117.6 2.1 %copy-start = (bf16[1920,8,128]{2,1,0:T(8,128)(2,1)S(1)}, bf16[1920,8,128]{2,1,0:T(8,128)(2,1)}, u32[]{:S(2)}) copy-start(bf16[1920,8,128]{2,1,0:T(8,128)(2,1)} %get-tuple-element.7) | copy-start | bytes 11796484
  119.7 1.1 copy-start.1
